TPU v7x, 32 devices: a whole 2x2x4 slice. The times are simulated.
32 devices in a mesh: row: 16 (over z, x, core), col: 2 (over y).
Axes of the slice: x: 2, y: 2, z: 4, core: 2. Of those that a mesh axis runs over, the one named last changes fastest.
Arguments:
- counts: float32 [8192, 8192], P('row', 'col'), may hold values from 0 to 12, as said below
- loadings: float32 [8192, 64], P(('col', 'row')), may hold values from 0.02 to 0.4
Outputs:
- row_grad: float32 [8192, 64], P(('row', 'col'))
- col_grad: float32 [8192, 64], P(('col', 'row'))
Inputs may be any that keep to these rules, and one draw needn't show every extreme that they name: `counts`: whole numbers, more of them near the diagonal.
All inputs are finite; a program needn't handle non-finite values.
Results may differ from a plain program's by a relative error of at most 0.0003.
Values sent between devices are 32-bit elements; how exact they have to be, the bound alone decides.
A program may use at most 64 MiB of HBM per device.

v0:
```python
import jax
import jax.numpy as jnp
from jax import lax
from jax.sharding import PartitionSpec as P


def broadcast(block, axis, source):
    block = jnp.where(lax.axis_index(axis) == source, block, jnp.zeros_like(block))
    return lax.psum(block, axis)


def shards(counts, loadings):
    rows = counts.shape[0]
    cols = counts.shape[1]
    nrow = lax.axis_size("row")
    ncol = lax.axis_size("col")
    nbins = rows * nrow
    scale = 1.0 / nbins**0.5
    row_index = lax.axis_index("row")
    col_index = lax.axis_index("col")
    colblock = lax.all_gather(loadings, "row", axis=0, tiled=True)
    group = nrow // ncol
    offset = row_index % group * rows
    portion = lax.dynamic_slice_in_dim(colblock, offset, rows, 0)
    rowblock = broadcast(portion, "col", row_index // group)
    rate = jnp.dot(rowblock, colblock.T, precision=lax.Precision.HIGHEST)
    positions = row_index * rows + jnp.arange(rows)
    targets = col_index * cols + jnp.arange(cols)
    keep = jnp.abs(positions[:, None] - targets[None, :]) >= 2
    ratio = jnp.where(keep, 1.0 - counts / rate, jnp.float32(0.0))
    slab = ratio
    row_grad = lax.psum_scatter(
        jnp.dot(slab, colblock, precision=lax.Precision.HIGHEST) * scale,
        "col",
        scatter_dimension=0,
        tiled=True,
    )
    slab = ratio
    col_grad = lax.psum_scatter(
        jnp.einsum("ij,ik->jk", slab, rowblock, precision=lax.Precision.HIGHEST) * scale,
        "row",
        scatter_dimension=0,
        tiled=True,
    )
    return (row_grad, col_grad)


def solution(mesh):
    placed = (P("row", "col"), P(("col", "row"), None))
    return jax.shard_map(
        shards,
        mesh=mesh,
        in_specs=placed,
        out_specs=(P(("row", "col"), None), P(("col", "row"), None)),
        check_vma=False,
    )
```

profile of v0, /device:TPU:0, one launch (start us, length us, event | category | flops | bytes accessed | tf_op | source)
XLA Modules:
  0.0 175.3 jit_solution(6677871117199778213)
XLA Ops:
  7.2 0.0 all-gather.2.cloned.1.call-start
  7.2 0.7 all-gather.2.cloned.1.call-update
  7.9 0.0 all-reduce.2.cloned.1.call-start
  8.0 41.6 %all-gather.2.cloned.1.call-done = f32[4096,64]{0,1:T(8,128)} async-done(((f32[256,64]{0,1:T(8,128)}), f32[4096,64]{0,1:T(8,128)}) %all-gather.2.cloned.1.call-update) | async-done | bytes 1048592 | tf_op jit(solution)/shard_map/all_gather | solution.py:21
  49.5 1.6 dynamic-slice_select_fusion
  51.1 0.0 all-reduce.2.cloned.1.call-update
  51.1 0.0 reduce-scatter.3.cloned.1.call-start
  51.2 0.0 copy-start.1
  51.2 21.7 %all-reduce.2.cloned.1.call-done = f32[512,64]{0,1:T(8,128)} async-done(((f32[512,64]{0,1:T(8,128)}), f32[512,64]{0,1:T(8,128)}) %all-reduce.2.cloned.1.call-update) | async-done | bytes 131088 | tf_op jit(solution)/shard_map/psum | solution.py:9
  73.0 11.5 %subtract_select_fusion = f32[512,4096]{1,0:T(8,128)S(1)} fusion(f32[512,4096]{1,0:T(8,128)} %param.2, f32[512,64]{0,1:T(8,128)} %all-reduce.2.cloned.1.call-done, f32[4096,64]{0,1:T(8,128)} %all-gather.2.cloned.1.call-done, s32[4096]{0:T(1024)S(1)} %iota_add_fusion, s32[512]{0:T(512)S(1)} %iota_add_fusion.1), kind=kOutput, calls=%fused_computation | convolution fusion | flops 1623195648 | bytes 17975296 | tf_op jit(solution)/shard_map/dot_general | solution.py:26
  84.5 0.0 copy-start
  84.5 3.2 %copy-done = f32[512,4096]{1,0:T(8,128)} copy-done((f32[512,4096]{1,0:T(8,128)}, f32[512,4096]{1,0:T(8,128)S(1)}, u32[]{:S(2)}) %copy-start) | copy-done | bytes 8388632
  87.7 0.0 copy-done.1
  87.7 0.0 copy-start.2
  87.7 8.9 %convolution_multiply_fusion.1 = f32[512,64]{0,1:T(8,128)} fusion(f32[512,4096]{1,0:T(8,128)S(1)} %subtract_select_fusion, f32[4096,64]{0,1:T(8,128)S(1)} %copy-done.1), kind=kOutput, calls=%fused_computation.3 | convolution fusion | flops 1610645504 | bytes 9568256 | tf_op jit(solution)/shard_map/dot_general | solution.py:33
  96.6 0.0 reduce-scatter.3.cloned.1.call-update
  96.6 0.2 reduce-scatter.5.cloned.1.call-start
  96.8 0.0 copy-done.2
  96.8 9.0 %convolution_multiply_fusion = f32[4096,64]{0,1:T(8,128)} fusion(f32[512,4096]{1,0:T(8,128)} %copy-done, f32[512,64]{0,1:T(8,128)S(1)} %copy-done.2), kind=kOutput, calls=%fused_computation.2 | convolution fusion | flops 1610874880 | bytes 9568256 | tf_op jit(solution)/shard_map/ij,ik->jk/dot_general | solution.py:40
  105.9 0.0 reduce-scatter.5.cloned.1.call-update
  105.9 1.2 reduce-scatter.3.cloned.1.call-done
  107.1 61.6 %reduce-scatter.5.cloned.1.call-done = f32[256,64]{0,1:T(8,128)} async-done(((f32[4096,64]{0,1:T(8,128)}), f32[256,64]{0,1:T(8,128)}) %reduce-scatter.5.cloned.1.call-update) | async-done | bytes 65552 | tf_op jit(solution)/shard_map/reduce_scatter | solution.py:39
  (2 shorter events, 0.0 us)
Async XLA Ops:
  7.2 42.4 %all-gather.2.cloned.1.call-start = ((), (), s32[]{:S(2)}) async-start(), calls=%async_computation.2 | async-start | bytes 1114112 | tf_op jit(solution)/shard_map/all_gather | solution.py:21
  7.9 65.1 %all-reduce.2.cloned.1.call-start = ((), (), s32[]{:S(2)}) async-start(), calls=%async_computation.3 | async-start | bytes 262144 | tf_op jit(solution)/shard_map/psum | solution.py:9
  51.1 56.0 %reduce-scatter.3.cloned.1.call-start = ((), (), s32[]{:S(2)}) async-start(), calls=%async_computation.4 | async-start | bytes 196608 | tf_op jit(solution)/shard_map/reduce_scatter | solution.py:32
  51.2 36.5 %copy-start.1 = (f32[4096,64]{0,1:T(8,128)S(1)}, f32[4096,64]{0,1:T(8,128)}, u32[]{:S(2)}) copy-start(f32[4096,64]{0,1:T(8,128)} %all-gather.2.cloned.1.call-done) | copy-start | bytes 3145732
  84.5 3.2 %copy-start = (f32[512,4096]{1,0:T(8,128)}, f32[512,4096]{1,0:T(8,128)S(1)}, u32[]{:S(2)}) copy-start(f32[512,4096]{1,0:T(8,128)S(1)} %subtract_select_fusion) | copy-start | bytes 25165828
  87.7 9.1 %copy-start.2 = (f32[512,64]{0,1:T(8,128)S(1)}, f32[512,64]{0,1:T(8,128)}, u32[]{:S(2)}) copy-start(f32[512,64]{0,1:T(8,128)} %all-reduce.2.cloned.1.call-done) | copy-start | bytes 393220
  96.6 72.2 %reduce-scatter.5.cloned.1.call-start = ((), (), s32[]{:S(2)}) async-start(), calls=%async_computation.5 | async-start | bytes 1114112 | tf_op jit(solution)/shard_map/reduce_scatter | solution.py:39
Sparse Core Ops, SparseCore 0:
  10.1 39.3 all-gather.1
  51.8 21.1 all-reduce.1
  96.7 10.3 reduce-scatter.2
  111.2 57.5 reduce-scatter.4
where the time goes:
time: 175 us
  waiting for transfers between devices  127 us (73%)
  matrix products  29.4 us (17%)
  between operations  13.8 us (8%)
  local copies, waits for them, and re-layouts  3.22 us (2%)
    reduce_scatter x1, waiting for transfers between devices, shards(): lax.psum_scatter(jnp.einsum('ij,ik->jk', slab, rowblock, precision=lax.Pr...  61.6 us
    all_gather x1, waiting for transfers between devices, shards(): colblock = lax.all_gather(loadings, 'row', axis=0, tiled=True)  41.6 us
    psum x1, waiting for transfers between devices, broadcast(): return lax.psum(block, axis)  21.7 us
    dot_general x1, matrix products, shards(): rate = jnp.dot(rowblock, colblock.T, precision=lax.Precision.HIGHEST)  11.5 us
    dot_general x1, matrix products, shards(): jnp.einsum('ij,ik->jk', slab, rowblock, precision=lax.Precision.HIGHEST)  9.02 us
    dot_general x1, matrix products, shards(): jnp.dot(slab, colblock, precision=lax.Precision.HIGHEST) * scale  8.88 us
  transfers between devices with their start and end apart: 4, of which 4 were waited for; matrix products, arithmetic and copies ran while one was open for 5% of the time, Pallas kernels for 0%

commit v1 on v0

--- a/solution.py
+++ b/solution.py
@@ -1,7 +1,15 @@
+import functools
+
 import jax
 import jax.numpy as jnp
 from jax import lax
+from jax.experimental import pallas as pl
+from jax.experimental.pallas import tpu as pltpu
 from jax.sharding import PartitionSpec as P
+
+MESH = pl.DeviceIdType.MESH
+NT = (((1,), (1,)), ((), ()))
+CHUNK = 256
 
 
 def broadcast(block, axis, source):
@@ -9,7 +17,7 @@
     return lax.psum(block, axis)
 
 
-def shards(counts, loadings):
+def plain(counts, loadings):
     rows = counts.shape[0]
     cols = counts.shape[1]
     nrow = lax.axis_size("row")
@@ -28,16 +36,14 @@
     targets = col_index * cols + jnp.arange(cols)
     keep = jnp.abs(positions[:, None] - targets[None, :]) >= 2
     ratio = jnp.where(keep, 1.0 - counts / rate, jnp.float32(0.0))
-    slab = ratio
     row_grad = lax.psum_scatter(
-        jnp.dot(slab, colblock, precision=lax.Precision.HIGHEST) * scale,
+        jnp.dot(ratio, colblock, precision=lax.Precision.HIGHEST) * scale,
         "col",
         scatter_dimension=0,
         tiled=True,
     )
-    slab = ratio
     col_grad = lax.psum_scatter(
-        jnp.einsum("ij,ik->jk", slab, rowblock, precision=lax.Precision.HIGHEST) * scale,
+        jnp.einsum("ij,ik->jk", ratio, rowblock, precision=lax.Precision.HIGHEST) * scale,
         "row",
         scatter_dimension=0,
         tiled=True,
@@ -45,7 +51,260 @@
     return (row_grad, col_grad)
 
 
+def split(value):
+    high = value.astype(jnp.bfloat16)
+    low = (value - high.astype(jnp.float32)).astype(jnp.bfloat16)
+    return high, low
+
+
+def flip(index, bit):
+    return index + bit - 2 * bit * (index // bit % 2)
+
+
+def flips(index, mask):
+    bit = 1
+    while bit <= mask:
+        if mask & bit:
+            index = flip(index, bit)
+        bit *= 2
+    return index
+
+
+def low_bit(mask):
+    return mask & -mask
+
+
+def kernel(
+    nrow, ncol, scale,
+    counts_ref, load_ref, row_out, col_out,
+    tiles, gathered, rowt, rowcat, rowhl, row_acc, parts, arrived, row_parts, row_arrived,
+    tile_sem, ag_send, ag_recv, rs_send, rs_recv, rb_send, rb_recv, rg_send, rg_recv,
+):
+    rows = counts_ref.shape[0]
+    own, rank = load_ref.shape
+    me = lax.axis_index("row")
+    mycol = lax.axis_index("col")
+    bits = []
+    bit = 1
+    while bit < nrow:
+        bits.append(bit)
+        bit *= 2
+
+    same = sorted((m for m in range(nrow) if not m & 1), key=lambda m: [m >> k & 1 for k in range(1, len(bits))])
+    other = [m | 1 for m in reversed(same)]
+    order = same + other
+
+    def tile_copy(m):
+        start = pl.multiple_of(flips(me, m) * own, own)
+        return pltpu.make_async_copy(counts_ref.at[:, pl.ds(start, own)], tiles.at[m], tile_sem.at[m])
+
+    for m in order:
+        tile_copy(m).start()
+
+    barrier = pltpu.get_barrier_semaphore()
+    for bit in bits:
+        pl.semaphore_signal(barrier, inc=1, device_id=(flip(me, bit), mycol), device_id_type=MESH)
+    for d in range(1, ncol):
+        pl.semaphore_signal(barrier, inc=1, device_id=(me, (mycol + d) % ncol), device_id_type=MESH)
+    for i in range(ncol):
+        block = me * ncol + i
+        source_row, source_col = block % nrow, block // nrow
+        pl.semaphore_signal(
+            barrier, inc=1, device_id=(source_row, source_col), device_id_type=MESH
+        )
+
+    gathered[0] = load_ref[...].T
+    pl.semaphore_wait(barrier, len(bits) + ncol - 1 + ncol)
+
+    mine = mycol * nrow + me
+    target, slot = mine // ncol, mine % ncol
+
+    def row_copy(c):
+        return pltpu.make_async_remote_copy(
+            gathered.at[0], rowt.at[slot], rb_send.at[c], rb_recv.at[slot],
+            device_id=(target, c), device_id_type=MESH,
+        )
+
+    def local_copy():
+        return pltpu.make_async_copy(gathered.at[0], rowt.at[slot], rb_recv.at[slot])
+
+    for c in range(ncol):
+        itself = (target == me) & (mycol == c)
+        pl.when(itself)(lambda: local_copy().start())
+        pl.when(jnp.logical_not(itself))(lambda c=c: row_copy(c).start())
+
+    def gather_copy(r):
+        bit = low_bit(r)
+        return pltpu.make_async_remote_copy(
+            gathered.at[r ^ bit], gathered.at[r], ag_send.at[r], ag_recv.at[r],
+            device_id=(flip(me, bit), mycol), device_id_type=MESH,
+        )
+
+    def forward(m):
+        if m:
+            gather_copy(m).wait_recv()
+        for bit in reversed(bits):
+            if m == 0 or bit < low_bit(m):
+                gather_copy(m | bit).start()
+
+    def reduce_copy(m):
+        bit = low_bit(m)
+        return pltpu.make_async_remote_copy(
+            parts.at[m], arrived.at[m], rs_send.at[m], rs_recv.at[m],
+            device_id=(flip(me, bit), mycol), device_id_type=MESH,
+        )
+
+    def finish(m):
+        total = parts[m]
+        for bit in bits:
+            if m == 0 or bit < low_bit(m):
+                reduce_copy(m | bit).wait_recv()
+                total += arrived[m | bit]
+        if m:
+            parts[m] = total
+            reduce_copy(m).start()
+        return total
+
+    def prepare_rows():
+        for i in range(ncol):
+            pltpu.make_async_remote_copy(
+                gathered.at[0], rowt.at[i], rb_send.at[0], rb_recv.at[i],
+                device_id=(me, mycol), device_id_type=MESH,
+            ).wait_recv()
+        for i in range(ncol):
+            high, low = split(rowt[i])
+            both = jnp.concatenate([high, low], axis=0)
+            rowhl[:, i * own:(i + 1) * own] = both
+            wide = jnp.concatenate([both, both], axis=0).astype(jnp.float32)
+            rowcat[i * own:(i + 1) * own, :] = wide.T.astype(jnp.bfloat16)
+
+    first_row = me * rows
+
+    def compute(m):
+        tile_copy(m).wait()
+        high, low = split(gathered[m])
+        colcat = jnp.concatenate([high, high, low, low], axis=0)
+        colhl = jnp.concatenate([high, low], axis=0)
+        first_col = (mycol * nrow + flips(me, m)) * own
+        total = None
+        for start in range(0, rows, CHUNK):
+            span = slice(start, start + CHUNK)
+            rate = jnp.dot(rowcat[span, :], colcat, preferred_element_type=jnp.float32)
+            guess = pl.reciprocal(rate, approx=True)
+            inverse = guess * (2.0 - rate * guess)
+            gap = (
+                lax.broadcasted_iota(jnp.int32, (CHUNK, own), 0)
+                - lax.broadcasted_iota(jnp.int32, (CHUNK, own), 1)
+                + (first_row + start - first_col)
+            )
+            ratio = jnp.where(jnp.abs(gap) >= 2, 1.0 - tiles[m, span, :] * inverse, 0.0)
+            high_r, low_r = split(ratio)
+            row_part = lax.dot_general(high_r, colhl, NT, preferred_element_type=jnp.float32)
+            row_part += lax.dot_general(low_r, colhl, NT, preferred_element_type=jnp.float32)
+            if m == order[0]:
+                row_acc[span, :] = row_part
+            else:
+                row_acc[span, :] += row_part
+            col_part = jnp.dot(rowhl[:, span], high_r, preferred_element_type=jnp.float32)
+            col_part += jnp.dot(rowhl[:, span], low_r, preferred_element_type=jnp.float32)
+            total = col_part if total is None else total + col_part
+        parts[m] = total[:rank] + total[rank:]
+        if m & 1:
+            reduce_copy(m).start()
+
+    forwards = list(same)
+    ahead = len(same) // 2
+    for m in forwards[:ahead]:
+        forward(m)
+    prepare_rows()
+    waiting = forwards[ahead:]
+    for m in same:
+        if waiting:
+            forward(waiting.pop(0))
+        compute(m)
+    passing = [m for m in reversed(same) if m & 2]
+    for k, m in enumerate(other):
+        gather_copy(m).wait_recv()
+        compute(m)
+        if k >= 2 and passing:
+            finish(passing.pop(0))
+    for m in passing:
+        finish(m)
+
+    sums = (row_acc[:, :rank] + row_acc[:, rank:]) * scale
+    for c in range(ncol):
+        row_parts[c] = sums[c * own:(c + 1) * own].T
+
+    def row_send(d):
+        to = (mycol + d) % ncol
+        return pltpu.make_async_remote_copy(
+            row_parts.at[to], row_arrived.at[d - 1], rg_send.at[d - 1], rg_recv.at[d - 1],
+            device_id=(me, to), device_id_type=MESH,
+        )
+
+    for d in range(1, ncol):
+        row_send(d).start()
+    for m in reversed(same):
+        if m and not m & 2:
+            finish(m)
+    row_total = row_parts[mycol]
+    for d in range(1, ncol):
+        row_send(d).wait_recv()
+        row_total += row_arrived[d - 1]
+    row_out[...] = row_total.T
+    col_out[...] = finish(0).T * scale
+
+    for m in range(1, nrow):
+        gather_copy(m).wait_send()
+        reduce_copy(m).wait_send()
+    for d in range(1, ncol):
+        row_send(d).wait_send()
+    for c in range(ncol):
+        itself = (target == me) & (mycol == c)
+        pl.when(jnp.logical_not(itself))(lambda c=c: row_copy(c).wait_send())
+
+
+def fused(nrow, ncol, counts, loadings):
+    rows = counts.shape[0]
+    own, rank = loadings.shape
+    f32, bf16 = jnp.float32, jnp.bfloat16
+    dma = pltpu.SemaphoreType.DMA
+    others = max(ncol - 1, 1)
+    return pl.pallas_call(
+        functools.partial(kernel, nrow, ncol, 1.0 / (rows * nrow) ** 0.5),
+        out_shape=(jax.ShapeDtypeStruct((own, rank), f32),) * 2,
+        in_specs=[pl.BlockSpec(memory_space=pl.ANY), pl.BlockSpec(memory_space=pltpu.VMEM)],
+        out_specs=(pl.BlockSpec(memory_space=pltpu.VMEM),) * 2,
+        scratch_shapes=[
+            pltpu.VMEM((nrow, rows, own), f32),
+            pltpu.VMEM((nrow, rank, own), f32),
+            pltpu.VMEM((ncol, rank, own), f32),
+            pltpu.VMEM((rows, 4 * rank), bf16),
+            pltpu.VMEM((2 * rank, rows), bf16),
+            pltpu.VMEM((rows, 2 * rank), f32),
+            pltpu.VMEM((nrow, rank, own), f32),
+            pltpu.VMEM((nrow, rank, own), f32),
+            pltpu.VMEM((ncol, rank, own), f32),
+            pltpu.VMEM((others, rank, own), f32),
+            dma((nrow,)), dma((nrow,)), dma((nrow,)), dma((nrow,)), dma((nrow,)),
+            dma((ncol,)), dma((ncol,)), dma((others,)), dma((others,)),
+        ],
+        compiler_params=pltpu.CompilerParams(
+            collective_id=0, has_side_effects=True, vmem_limit_bytes=60 * 2**20
+        ),
+    )(counts, loadings)
+
+
 def solution(mesh):
+    nrow, ncol = mesh.shape["row"], mesh.shape["col"]
+
+    def shards(counts, loadings):
+        rows = counts.shape[0]
+        own, rank = loadings.shape
+        fits = nrow >= 4 and nrow & (nrow - 1) == 0 and rows == own * ncol
+        fits = fits and own % 128 == 0 and rank % 64 == 0 and rows % CHUNK == 0
+        return fused(nrow, ncol, counts, loadings) if fits else plain(counts, loadings)
+
     placed = (P("row", "col"), P(("col", "row"), None))
     return jax.shard_map(
         shards,

time: 175 us -> 46.1 us (0.26)
  waiting for transfers between devices: 127 us -> 0 us
  Pallas kernels: 0 us -> 40.4 us
  matrix products: 29.4 us -> 0 us
  between operations: 13.8 us -> 0.64 us
    reduce_scatter x2 -> x0, waiting for transfers between devices: 62.9 us -> none  [the longest x1 61.6 us: shards(): lax.psum_scatter(jnp.einsum('ij,ik->jk', slab, rowblock, precision=lax.Pr...]
    all_gather x1 -> x0, waiting for transfers between devices: 41.6 us -> none  [shards(): colblock = lax.all_gather(loadings, 'row', axis=0, tiled=True)]
    pallas_call x0 -> x1, Pallas kernels: none -> 40.4 us  [fused(): pl.pallas_call(functools.partial(kernel, nrow, ncol, 1.0 / (rows * nrow)...]
    dot_general x3 -> x0, matrix products: 29.4 us -> none  [the longest x1 11.5 us: shards(): rate = jnp.dot(rowblock, colblock.T, precision=lax.Precision.HIGHEST)]
    psum x1 -> x0, waiting for transfers between devices: 21.7 us -> none  [broadcast(): return lax.psum(block, axis)]
    pallas_call x0 -> x2, local copies, waits for them, and re-layouts: none -> 3.23 us  [fused(): pl.pallas_call(functools.partial(kernel, nrow, ncol, 1.0 / (rows * nrow)...]
  transfers between devices with their start and end apart: 4 -> 0, of which waited for: 4 -> 0; matrix products, arithmetic and copies ran while one was open for 5% -> 0% of each run, Pallas kernels for 0% -> 0%
where the time goes in v1:
time: 46.1 us; the launch traced here: 45.9 us
  Pallas kernels  40.4 us (88%)
  local copies, waits for them, and re-layouts  4.82 us (10%)
  between operations  0.64 us (1%)
    pallas_call x1, Pallas kernels, fused(): pl.pallas_call(functools.partial(kernel, nrow, ncol, 1.0 / (rows * nrow)...  40.4 us
    pallas_call x2, local copies, waits for them, and re-layouts, fused(): pl.pallas_call(functools.partial(kernel, nrow, ncol, 1.0 / (rows * nrow)...  3.23 us
    unnamed x1, local copies, waits for them, and re-layouts  1.59 us

profile of v1, /device:TPU:0, one launch (start us, length us, event | category | flops | bytes accessed | tf_op | source)
XLA Modules:
  0.0 45.9 jit_solution(10705496114904190268)
XLA Ops:
  0.6 1.6 %copy.4.load_ref = f32[256,64]{1,0:T(8,128)} copy(f32[256,64]{0,1:T(8,128)} %param.3) | data formatting | bytes 131072 | tf_op args[1]
  2.2 40.4 %shard_map.41 = (f32[256,64]{1,0:T(8,128)}, f32[256,64]{1,0:T(8,128)}) custom-call(f32[512,4096]{1,0:T(8,128)} %counts_ref.1, f32[256,64]{1,0:T(8,128)} %copy.4.load_ref), custom_call_target="tpu_custom_call" | custom-call | tf_op jit(solution)/shard_map/pallas_call | solution.py:273
  42.6 1.6 %copy.5 = f32[256,64]{0,1:T(8,128)} copy(f32[256,64]{1,0:T(8,128)} %get-tuple-element.2) | data formatting | bytes 131072 | tf_op jit(solution)/shard_map/pallas_call | solution.py:273
  44.2 1.6 %copy.6 = f32[256,64]{0,1:T(8,128)} copy(f32[256,64]{1,0:T(8,128)} %get-tuple-element.3) | data formatting | bytes 131072 | tf_op jit(solution)/shard_map/pallas_call | solution.py:273

commit v2 on v1

--- a/solution.py
+++ b/solution.py
@@ -78,10 +78,10 @@
     nrow, ncol, scale,
     counts_ref, load_ref, row_out, col_out,
     tiles, gathered, rowt, rowcat, rowhl, row_acc, parts, arrived, row_parts, row_arrived,
-    tile_sem, ag_send, ag_recv, rs_send, rs_recv, rb_send, rb_recv, rg_send, rg_recv,
+    load_sem, tile_sem, ag_send, ag_recv, rs_send, rs_recv, rb_send, rb_recv, rg_send, rg_recv,
 ):
     rows = counts_ref.shape[0]
-    own, rank = load_ref.shape
+    rank, own = load_ref.shape
     me = lax.axis_index("row")
     mycol = lax.axis_index("col")
     bits = []
@@ -98,8 +98,8 @@
         start = pl.multiple_of(flips(me, m) * own, own)
         return pltpu.make_async_copy(counts_ref.at[:, pl.ds(start, own)], tiles.at[m], tile_sem.at[m])
 
-    for m in order:
-        tile_copy(m).start()
+    fetch = pltpu.make_async_copy(load_ref, gathered.at[0], load_sem)
+    fetch.start()
 
     barrier = pltpu.get_barrier_semaphore()
     for bit in bits:
@@ -113,7 +113,9 @@
             barrier, inc=1, device_id=(source_row, source_col), device_id_type=MESH
         )
 
-    gathered[0] = load_ref[...].T
+    for m in order:
+        tile_copy(m).start()
+    fetch.wait()
     pl.semaphore_wait(barrier, len(bits) + ncol - 1 + ncol)
 
     mine = mycol * nrow + me
@@ -251,8 +253,8 @@
     for d in range(1, ncol):
         row_send(d).wait_recv()
         row_total += row_arrived[d - 1]
-    row_out[...] = row_total.T
-    col_out[...] = finish(0).T * scale
+    row_out[...] = row_total
+    col_out[...] = finish(0) * scale
 
     for m in range(1, nrow):
         gather_copy(m).wait_send()
@@ -270,10 +272,10 @@
     f32, bf16 = jnp.float32, jnp.bfloat16
     dma = pltpu.SemaphoreType.DMA
     others = max(ncol - 1, 1)
-    return pl.pallas_call(
+    row_grad, col_grad = pl.pallas_call(
         functools.partial(kernel, nrow, ncol, 1.0 / (rows * nrow) ** 0.5),
-        out_shape=(jax.ShapeDtypeStruct((own, rank), f32),) * 2,
-        in_specs=[pl.BlockSpec(memory_space=pl.ANY), pl.BlockSpec(memory_space=pltpu.VMEM)],
+        out_shape=(jax.ShapeDtypeStruct((rank, own), f32),) * 2,
+        in_specs=[pl.BlockSpec(memory_space=pl.ANY)] * 2,
         out_specs=(pl.BlockSpec(memory_space=pltpu.VMEM),) * 2,
         scratch_shapes=[
             pltpu.VMEM((nrow, rows, own), f32),
@@ -286,13 +288,14 @@
             pltpu.VMEM((nrow, rank, own), f32),
             pltpu.VMEM((ncol, rank, own), f32),
             pltpu.VMEM((others, rank, own), f32),
-            dma((nrow,)), dma((nrow,)), dma((nrow,)), dma((nrow,)), dma((nrow,)),
+            dma, dma((nrow,)), dma((nrow,)), dma((nrow,)), dma((nrow,)), dma((nrow,)),
             dma((ncol,)), dma((ncol,)), dma((others,)), dma((others,)),
         ],
         compiler_params=pltpu.CompilerParams(
             collective_id=0, has_side_effects=True, vmem_limit_bytes=60 * 2**20
         ),
-    )(counts, loadings)
+    )(counts, loadings.T)
+    return row_grad.T, col_grad.T
 
 
 def solution(mesh):

time: 46.1 us -> 43.3 us (0.939)
  local copies, waits for them, and re-layouts: 4.82 us -> 2.95 us
  Pallas kernels: 40.4 us -> 39.5 us
    pallas_call x2 -> x0, local copies, waits for them, and re-layouts: 3.23 us -> none  [fused(): pl.pallas_call(functools.partial(kernel, nrow, ncol, 1.0 / (rows * nrow)...]
    unnamed x1 -> x2, local copies, waits for them, and re-layouts: 1.59 us -> 2.95 us
    pallas_call x1, Pallas kernels: 40.4 us -> 39.5 us  [fused(): pl.pallas_call(functools.partial(kernel, nrow, ncol, 1.0 / (rows * nrow)...]
where the time goes in v2:
time: 43.3 us; the launch traced here: 43.1 us
  Pallas kernels  39.5 us (91%)
  local copies, waits for them, and re-layouts  2.95 us (7%)
  between operations  0.64 us (1%)
    pallas_call x1, Pallas kernels, fused(): pl.pallas_call(functools.partial(kernel, nrow, ncol, 1.0 / (rows * nrow)...  39.5 us
    unnamed x2, local copies, waits for them, and re-layouts  2.95 us

profile of v2, /device:TPU:0, one launch (start us, length us, event | category | flops | bytes accessed | tf_op | source)
XLA Modules:
  0.0 43.1 jit_solution(4865279910145754035)
XLA Ops:
  0.6 39.5 %shard_map.41 = (f32[64,256]{1,0:T(8,128)}, f32[64,256]{1,0:T(8,128)}) custom-call(f32[512,4096]{1,0:T(8,128)} %counts_ref.1, f32[64,256]{1,0:T(8,128)} %bitcast.3), custom_call_target="tpu_custom_call" | custom-call | tf_op jit(solution)/shard_map/pallas_call | solution.py:275
  40.2 1.5 %copy.6 = f32[256,64]{0,1:T(8,128)} copy(f32[256,64]{0,1:T(8,128)} %bitcast.5) | data formatting | bytes 131072
  41.6 1.5 %copy.7 = f32[256,64]{0,1:T(8,128)} copy(f32[256,64]{0,1:T(8,128)} %bitcast.4) | data formatting | bytes 131072

commit v3 on v2

--- a/solution.py
+++ b/solution.py
@@ -130,10 +130,11 @@
     def local_copy():
         return pltpu.make_async_copy(gathered.at[0], rowt.at[slot], rb_recv.at[slot])
 
-    for c in range(ncol):
-        itself = (target == me) & (mycol == c)
-        pl.when(itself)(lambda: local_copy().start())
-        pl.when(jnp.logical_not(itself))(lambda c=c: row_copy(c).start())
+    def start_rows():
+        for c in range(ncol):
+            itself = (target == me) & (mycol == c)
+            pl.when(itself)(lambda: local_copy().start())
+            pl.when(jnp.logical_not(itself))(lambda c=c: row_copy(c).start())
 
     def gather_copy(r):
         bit = low_bit(r)
@@ -215,9 +216,11 @@
             reduce_copy(m).start()
 
     forwards = list(same)
-    ahead = len(same) // 2
+    ahead = max(len(same) * 3 // 8, 1)
     for m in forwards[:ahead]:
         forward(m)
+        if m == 0:
+            start_rows()
     prepare_rows()
     waiting = forwards[ahead:]
     for m in same:

time: 43.3 us -> 40.1 us (0.926)
  Pallas kernels: 39.5 us -> 36.3 us
    pallas_call x1, Pallas kernels: 39.5 us -> 36.3 us  [fused(): pl.pallas_call(functools.partial(kernel, nrow, ncol, 1.0 / (rows * nrow)...]
where the time goes in v3:
time: 40.1 us; the launch traced here: 39.9 us
  Pallas kernels  36.3 us (91%)
  local copies, waits for them, and re-layouts  2.95 us (7%)
  between operations  0.64 us (2%)
    pallas_call x1, Pallas kernels, fused(): pl.pallas_call(functools.partial(kernel, nrow, ncol, 1.0 / (rows * nrow)...  36.3 us
    unnamed x2, local copies, waits for them, and re-layouts  2.95 us

profile of v3, /device:TPU:0, one launch (start us, length us, event | category | flops | bytes accessed | tf_op | source)
XLA Modules:
  0.0 39.9 jit_solution(8970304264348275169)
XLA Ops:
  0.6 36.3 %shard_map.41 = (f32[64,256]{1,0:T(8,128)}, f32[64,256]{1,0:T(8,128)}) custom-call(f32[512,4096]{1,0:T(8,128)} %counts_ref.1, f32[64,256]{1,0:T(8,128)} %bitcast.3), custom_call_target="tpu_custom_call" | custom-call | tf_op jit(solution)/shard_map/pallas_call | solution.py:278
  36.9 1.5 %copy.6 = f32[256,64]{0,1:T(8,128)} copy(f32[256,64]{0,1:T(8,128)} %bitcast.5) | data formatting | bytes 131072
  38.4 1.5 %copy.7 = f32[256,64]{0,1:T(8,128)} copy(f32[256,64]{0,1:T(8,128)} %bitcast.4) | data formatting | bytes 131072
